TPU v7x, 512 devices: a whole 4x4x16 slice. The times are simulated.
512 devices in a mesh: sector: 64 (over z, y_lo, core), radial: 8 (over x, y_hi).
Axes of the slice: x: 4, y: 4 (y_hi: 2, y_lo: 2; y = y_hi * 2 + y_lo), z: 16, core: 2. Of those that a mesh axis runs over, the one named last changes fastest.
Arguments:
- fields: float32 [64, 8, 140, 1024], P('sector', 'radial'), may hold values from -6 to 6
- pattern: int32 [64, 8, 1024], P('sector', 'radial'), may hold values from 0 to 15
- tent_order: int32 [64, 8, 1024], P('sector', 'radial'), may hold values from 0 to 1023, each once within a row
- level_sizes: int32 [64, 8, 4], P('sector', 'radial'), may hold values from 1 to 384, 1024 in all within a row
- send_rows: int32 [64, 8, 4, 128], P('sector', 'radial'), may hold values from 0 to 1023
- neighbours: int32 [64, 8, 4, 1024], P('sector', 'radial'), may hold values from 0 to 1535, as said below
- operator: float32 [140, 140], replicated, may hold values from -2 to 2, as said below
- trace_map: float32 [60, 140], replicated, may hold values from -0.5 to 0.5
- lift_map: float32 [4, 140, 60], replicated, may hold values from -0.375 to 0.375
- tent_height: float32 [16], replicated, may hold values from 0.15 to 0.5
Outputs:
- advanced: float32 [64, 8, 140, 1024], P('sector', 'radial')
Inputs may be any that keep to these rules, and one draw needn't show every extreme that they name: `tent_order`: each block's entries are a permutation of 0 to 1023. `level_sizes`: each block's 4 sizes sum to 1024, and some level of every block has exactly 384 tents. `neighbours`: an entry below 1024 names an element of the same block; an entry 1024 + d * 128 + j names the j-th received trace of group d of extended; each of these 512 slots is named by face 0 of exactly one element of the block. `operator`: a skew-symmetric matrix minus a diagonal of positive damping rates.
All inputs are finite; a program needn't handle non-finite values.
Results may differ from a plain program's by a relative error of at most 0.0003.
Values sent between devices are 32-bit elements; how exact they have to be, the bound alone decides.
A program may use at most 64 MiB of HBM per device.

v0:
```python
import functools

import jax
import jax.numpy as jnp
import numpy as np
from jax import lax
from jax.experimental import pallas as pl
from jax.experimental.pallas import tpu as pltpu
from jax.sharding import PartitionSpec as P

LEVELS = 4
FACES = 4
SUBSTEPS = 2
TERMS = 4
BLOCK = 384
ELEMS = 1024
COMP = 140
TRACE = 60
BND = 128
CP = 144
TP = 64
LOCAL = LEVELS * BLOCK
KB = 256

MESH = pl.DeviceIdType.MESH
F32 = jnp.float32
BF16 = jnp.bfloat16
I32 = jnp.int32


def substep_powers():
    one = np.array([1.0 / np.prod(np.arange(1, k + 1)) for k in range(TERMS + 1)])
    total = np.array([1.0])
    for _ in range(SUBSTEPS):
        total = np.convolve(total, one)
    return [float(c) for c in total]


COEF = substep_powers()
DEG = SUBSTEPS * TERMS


def hi_lo(x):
    hi = x.astype(BF16)
    return hi, (x - hi.astype(F32)).astype(BF16)


def right3(x):
    hi, lo = hi_lo(x)
    return jnp.concatenate([hi, hi, lo], axis=0)


def left3(m):
    hi, lo = hi_lo(m)
    return jnp.concatenate([hi, lo, hi], axis=1)


def dot(a, b):
    return jnp.dot(a, b, preferred_element_type=F32)


def dot_exact(a, b):
    return jnp.dot(a, b, precision=lax.Precision.HIGHEST, preferred_element_type=F32)


def one_hot(row, depth):
    n = row.shape[1]
    line = lax.broadcasted_iota(I32, (depth, n), 0)
    return jnp.where(line == jnp.broadcast_to(row, (depth, n)), 1.0, 0.0).astype(BF16)


def look_up(table, index):
    lane = index & 127
    tile = index >> 7
    out = jnp.zeros(index.shape, table.dtype)
    for m in range(table.shape[1] // 128):
        part = jnp.broadcast_to(table[:, 128 * m : 128 * m + 128], index.shape)
        got = jnp.take_along_axis(part, lane, axis=1, mode="promise_in_bounds")
        out = jnp.where(tile == m, got, out)
    return out


def kernel(
    secs,
    rads,
    fields,
    pattern,
    order,
    sizes,
    neighbours,
    sends,
    operator,
    trace_map,
    lift_map,
    tent_height,
    out,
    xp,
    tp,
    ap,
    lp,
    t3,
    a3,
    l3,
    ohin,
    pos_ref,
    sx_ref,
    nbx_ref,
    h_ref,
    state,
    flow,
    gath,
    loaded_ref,
    sb,
    rb,
    send_sem,
    recv_sem,
):
    s = lax.axis_index("sector")
    r = lax.axis_index("radial")
    up = lax.rem(s + 1, secs)
    down = lax.rem(s + secs - 1, secs)

    barrier = pltpu.get_barrier_semaphore()

    def greet(a, b):
        pl.semaphore_signal(barrier, inc=1, device_id=(a, b), device_id_type=MESH)

    greet(up, r)
    greet(down, r)

    @pl.when(r > 0)
    def _():
        greet(s, r - 1)

    @pl.when(r < rads - 1)
    def _():
        greet(s, r + 1)

    @pl.when(r == 0)
    def _():
        rb[:, 2] = jnp.zeros((LEVELS, TP, BND), F32)

    @pl.when(r == rads - 1)
    def _():
        rb[:, 3] = jnp.zeros((LEVELS, TP, BND), F32)

    def copy(level, group, a, b):
        return pltpu.make_async_remote_copy(
            src_ref=sb.at[level, group],
            dst_ref=rb.at[level, group],
            send_sem=send_sem.at[level, group],
            recv_sem=recv_sem.at[level, group],
            device_id=(a, b),
            device_id_type=MESH,
        )

    def start(level):
        @pl.when(r < rads - 1)
        def _():
            copy(level, 2, s, r + 1).start()

        @pl.when(r > 0)
        def _():
            copy(level, 3, s, r - 1).start()

        copy(level, 0, up, r).start()
        copy(level, 1, down, r).start()

    def arrive(level):
        copy(level, 0, up, r).wait_recv()
        copy(level, 1, down, r).wait_recv()

        @pl.when(r > 0)
        def _():
            copy(level, 2, s, r - 1).wait_recv()

        @pl.when(r < rads - 1)
        def _():
            copy(level, 3, s, r + 1).wait_recv()

    def drain(level):
        copy(level, 0, up, r).wait_send()
        copy(level, 1, down, r).wait_send()

        @pl.when(r < rads - 1)
        def _():
            copy(level, 2, s, r + 1).wait_send()

        @pl.when(r > 0)
        def _():
            copy(level, 3, s, r - 1).wait_send()

    def fill_sends(level, got):
        for d in range(4):
            part = got[:, BND * d : BND * d + BND]
            sb[level, d] = part[:TP] + part[TP:]

    tp[...] = jnp.zeros((TP, CP), F32)
    tp[0:TRACE, 0:COMP] = trace_map[...]
    t3[0:TP] = left3(tp[...])
    xp[0:COMP] = fields[...]
    xp[COMP:CP] = jnp.zeros((CP - COMP, ELEMS), F32)
    first = dot(t3[0:TP], right3(xp[...]))
    first_hl = jnp.concatenate(hi_lo(first), axis=0)
    got = jnp.zeros((2 * TP, 4 * BND), F32)
    for m in range(ELEMS // KB):
        got += dot(first_hl[:, KB * m : KB * m + KB], one_hot(sends[...] - KB * m, KB))
    fill_sends(0, got)
    pl.semaphore_wait(
        barrier, 2 + jnp.where(r > 0, 1, 0) + jnp.where(r < rads - 1, 1, 0)
    )
    start(0)

    ap[...] = jnp.zeros((CP, CP), F32)
    ap[0:COMP, 0:COMP] = operator[...]
    p1 = ap[...]
    p2 = dot_exact(p1, p1)
    p12 = jnp.concatenate([p1, p2], axis=0)
    p34 = dot_exact(p12, p2)
    p4 = p34[CP:]
    p14 = jnp.concatenate([p12, p34], axis=0)
    p58 = dot_exact(p14, p4)
    a3[0 : 4 * CP] = left3(p14)
    a3[4 * CP :] = left3(p58)
    q0 = tp[...]
    q1 = dot_exact(q0, p1)
    q01 = jnp.concatenate([q0, q1], axis=0)
    q23 = dot_exact(q01, p2)
    q03 = jnp.concatenate([q01, q23], axis=0)
    q47 = dot_exact(q03, p4)
    q8 = dot_exact(q47[:TP], p4)
    t3[TP:] = left3(jnp.concatenate([q1, q23, q47, q8], axis=0))
    lp[...] = jnp.zeros((CP, FACES * TP), F32)
    for f in range(FACES):
        lp[0:COMP, TP * f : TP * f + TRACE] = lift_map[f]
    l3[...] = left3(lp[...])

    line = lax.broadcasted_iota(I32, (16, 128), 0)
    lane = lax.broadcasted_iota(I32, (16, 128), 1)
    shift = jnp.zeros((16, 128), I32)
    limit = jnp.zeros((16, 128), I32)
    begin = jnp.int32(0)
    for l in range(LEVELS):
        size = sizes[l]
        mine = (line >= 3 * l) & (line < 3 * l + 3)
        shift = jnp.where(mine, begin - BLOCK * l, shift)
        limit = jnp.where(mine, BLOCK * l + size, limit)
        begin = begin + size
    slot = 128 * line + lane
    place = jnp.minimum(jnp.maximum(slot + shift, 0), ELEMS - 1)
    element = jnp.where(slot < limit, look_up(order[...], place), -1)
    for l in range(LEVELS):
        row = jnp.concatenate([element[3 * l + t : 3 * l + t + 1] for t in range(3)], axis=1)
        for m in range(ELEMS // KB):
            ohin[l, KB * m : KB * m + KB] = one_hot(row - KB * m, KB)

    line = lax.broadcasted_iota(I32, (16, BLOCK), 0)
    lane = lax.broadcasted_iota(I32, (16, BLOCK), 1)
    pos = jnp.zeros((16, ELEMS), F32)
    for l in range(LEVELS):
        number = lane + BLOCK * l
        digits = jnp.where(line == 0, number >> 8, jnp.where(line == 1, number & 255, 0))
        pos += lax.dot_general(
            digits.astype(F32).astype(BF16),
            ohin[l],
            (((1,), (1,)), ((), ())),
            preferred_element_type=F32,
        )
    pos = pos.astype(I32)
    pos = pos[0:1] * 256 + pos[1:2]
    pos_ref[...] = pos

    wide = []
    for t in range(ELEMS // 128):
        part = neighbours[:, 128 * t : 128 * t + 128]
        inside = look_up(pos, jnp.minimum(part, ELEMS - 1))
        wide.append(jnp.where(part < ELEMS, inside, part + (LOCAL - ELEMS)))
    wide = jnp.concatenate(wide, axis=1)
    for d in range(4):
        sx_ref[:, BND * d : BND * d + BND] = look_up(
            pos, jnp.broadcast_to(sends[:, BND * d : BND * d + BND], (8, BND))
        )[0:1]

    line = lax.broadcasted_iota(I32, (8, ELEMS), 0)
    extra = jnp.where(line == 0, jnp.broadcast_to(pattern[...], (8, ELEMS)), 0)
    index_rows = jnp.concatenate([wide >> 8, wide & 255, extra], axis=0)
    xhi, xlo = hi_lo(xp[...])
    rows = jnp.concatenate([xhi, xlo, index_rows.astype(F32).astype(BF16)], axis=0)
    for l in range(LEVELS):
        moved = dot(rows, ohin[l])
        x = moved[:CP] + moved[CP : 2 * CP]
        state[l] = x
        numbers = moved[2 * CP :].astype(I32)
        nbx_ref[l] = numbers[0:4] * 256 + numbers[4:8]
        kind = numbers[8:9]
        height = jnp.zeros((1, BLOCK), F32)
        for p in range(16):
            height = jnp.where(kind == p, tent_height[p], height)
        h_ref[l] = height
        o = dot(t3[0:TP], right3(x))
        flow[:, BLOCK * l : BLOCK * l + BLOCK] = jnp.concatenate(hi_lo(o), axis=0)
    out[...] = jnp.zeros((COMP, ELEMS), F32)

    def weights(l):
        h = h_ref[l]
        power = jnp.ones_like(h)
        ws = []
        for k in range(1, DEG + 1):
            power = power * h
            ws.append(power * COEF[k])
        return ws

    def finish(l):
        x = loaded_ref[...]
        x3 = right3(x)
        y = x
        ws = weights(l)
        for k in range(1, DEG + 1):
            y += dot(a3[CP * (k - 1) : CP * k], x3) * ws[k - 1]
        hl = jnp.concatenate(hi_lo(y), axis=0)
        for n in range(ELEMS // KB):
            row = pos_ref[:, KB * n : KB * n + KB] - BLOCK * l
            got = dot(hl, one_hot(row, BLOCK))
            out[:, KB * n : KB * n + KB] += got[:COMP] + got[CP : CP + COMP]

    def level(l, carry):
        @pl.when(l > 0)
        def _():
            finish(l - 1)

        for f in range(FACES):
            row = nbx_ref[l, f : f + 1]
            acc = jnp.zeros((2 * TP, BLOCK), F32)
            for m in range(LOCAL // KB):
                acc += dot(flow[:, KB * m : KB * m + KB], one_hot(row - KB * m, KB))
            gath[f] = acc
        arrive(l)
        for d in range(4):
            hi, lo = hi_lo(rb[l, d])
            flow[:, LOCAL + BND * d : LOCAL + BND * d + BND] = jnp.concatenate([hi, lo], axis=0)
        his, los = [], []
        for f in range(FACES):
            row = nbx_ref[l, f : f + 1]
            acc = gath[f]
            for m in range(LOCAL // KB, (LOCAL + 4 * BND) // KB):
                acc += dot(flow[:, KB * m : KB * m + KB], one_hot(row - KB * m, KB))
            acc = acc.astype(BF16)
            his.append(acc[:TP])
            los.append(acc[TP:])
        x = state[l] + dot(l3[...], jnp.concatenate(his + his + los, axis=0))
        loaded_ref[...] = x

        @pl.when(l < LEVELS - 1)
        def _():
            x3 = right3(x)
            ws = weights(l)
            o = dot(t3[0:TP], x3)
            for k in range(1, DEG + 1):
                o += dot(t3[TP * k : TP * k + TP], x3) * ws[k - 1]
            here = pl.ds(pl.multiple_of(BLOCK * l, 128), BLOCK)
            flow[:, here] = jnp.concatenate(hi_lo(o), axis=0)
            got = jnp.zeros((2 * TP, 4 * BND), F32)
            for m in range(LOCAL // KB):
                got += dot(flow[:, KB * m : KB * m + KB], one_hot(sx_ref[...] - KB * m, KB))
            fill_sends(l + 1, got)
            start(l + 1)

        return carry

    lax.fori_loop(0, LEVELS, level, 0)
    finish(LEVELS - 1)
    for l in range(LEVELS):
        drain(l)


def solution(mesh):
    secs, rads = mesh.shape["sector"], mesh.shape["radial"]
    vmem = pl.BlockSpec(memory_space=pltpu.VMEM)
    smem = pl.BlockSpec(memory_space=pltpu.SMEM)

    def body(
        fields,
        pattern,
        tent_order,
        level_sizes,
        send_rows,
        neighbours,
        operator,
        trace_map,
        lift_map,
        tent_height,
    ):
        out = pl.pallas_call(
            functools.partial(kernel, secs, rads),
            out_shape=jax.ShapeDtypeStruct((COMP, ELEMS), F32),
            in_specs=[vmem, vmem, vmem, smem, vmem, vmem, vmem, vmem, vmem, smem],
            out_specs=vmem,
            scratch_shapes=[
                pltpu.VMEM((CP, ELEMS), F32),
                pltpu.VMEM((TP, CP), F32),
                pltpu.VMEM((CP, CP), F32),
                pltpu.VMEM((CP, FACES * TP), F32),
                pltpu.VMEM(((DEG + 1) * TP, 3 * CP), BF16),
                pltpu.VMEM((DEG * CP, 3 * CP), BF16),
                pltpu.VMEM((CP, 3 * FACES * TP), BF16),
                pltpu.VMEM((LEVELS, ELEMS, BLOCK), BF16),
                pltpu.VMEM((1, ELEMS), I32),
                pltpu.VMEM((1, 4 * BND), I32),
                pltpu.VMEM((LEVELS, 4, BLOCK), I32),
                pltpu.VMEM((LEVELS, 1, BLOCK), F32),
                pltpu.VMEM((LEVELS, CP, BLOCK), F32),
                pltpu.VMEM((2 * TP, LOCAL + 4 * BND), BF16),
                pltpu.VMEM((FACES, 2 * TP, BLOCK), F32),
                pltpu.VMEM((CP, BLOCK), F32),
                pltpu.VMEM((LEVELS, 4, TP, BND), F32),
                pltpu.VMEM((LEVELS, 4, TP, BND), F32),
                pltpu.SemaphoreType.DMA((LEVELS, 4)),
                pltpu.SemaphoreType.DMA((LEVELS, 4)),
            ],
            compiler_params=pltpu.CompilerParams(
                collective_id=0, has_side_effects=True, vmem_limit_bytes=60 * 2**20
            ),
            name="tent_layer",
        )(
            fields[0, 0],
            pattern[0],
            tent_order[0],
            level_sizes[0, 0],
            neighbours[0, 0],
            send_rows.reshape(1, 4 * BND),
            operator,
            trace_map,
            lift_map,
            tent_height,
        )
        return out[None, None]

    block = P("sector", "radial", None)
    wide = P("sector", "radial", None, None)
    return jax.shard_map(
        body,
        mesh=mesh,
        in_specs=(wide, block, block, block, wide, wide, P(), P(), P(), P()),
        out_specs=wide,
        check_vma=False,
    )
```

profile of v0, /device:TPU:2, one launch (start us, length us, event | category | flops | bytes accessed | tf_op | source)
XLA Modules:
  0.0 47.3 jit_solution(16912757299055505465)
XLA Ops:
  0.0 1.8 %copy.11.lift_map = f32[4,140,60]{2,1,0:T(8,128)} copy(f32[4,140,60]{1,0,2:T(4,128)} %param.18) | data formatting | bytes 268800 | tf_op args[8]
  1.8 2.0 %copy.15 = f32[1,1,140,1024]{3,2,1,0:T(8,128)} copy(f32[1,1,140,1024]{3,1,2,0:T(1,128)} %param.10) | data formatting | bytes 1146880
  3.8 41.0 %tent_layer.1 = f32[140,1024]{1,0:T(8,128)} custom-call(f32[140,1024]{1,0:T(8,128)} %bitcast.10, s32[1,1024]{1,0:T(1,128)} %bitcast.12, s32[1,1024]{1,0:T(1,128)} %bitcast.13, s32[4]{0:T(128)} %bitcast.15, s32[4,1024]{1,0:T(4,128)} %bitcast.11, s32[1,512]{1,0:T(1,128)} %bitcast.14, f32[140,140]{1,0:T(8,128)} %operator.1, f32[60,140]{1,0:T(8,128)} %trace_map.1, ...), custom_call_target="tpu_custom_call" | custom-call | tf_op jit(solution)/shard_map/tent_layer/pallas_call | solution.py:393
  44.8 2.5 %copy.12 = f32[1,1,140,1024]{3,1,2,0:T(1,128)} copy(f32[1,1,140,1024]{3,2,1,0:T(8,128)} %bitcast.9) | data formatting | bytes 1146880 | tf_op jit(solution)/shard_map/broadcast_in_dim | solution.py:436
where the time goes:
time: 47.5 us; the launch traced here: 47.3 us
  Pallas kernels  41 us (86%)
  local copies, waits for them, and re-layouts  6.28 us (13%)
    pallas_call x1, Pallas kernels, body(): pl.pallas_call(functools.partial(kernel, secs, rads), out_shape=jax.Shape...  41 us
    unnamed x2, local copies, waits for them, and re-layouts  3.81 us
    broadcast_in_dim x1, local copies, waits for them, and re-layouts, body(): return out[None, None]  2.46 us

commit v1 on v0

v1 whole, which is shorter than its diff:
```python
import functools

import jax
import jax.numpy as jnp
import numpy as np
from jax import lax
from jax.experimental import pallas as pl
from jax.experimental.pallas import tpu as pltpu
from jax.sharding import PartitionSpec as P

LEVELS = 4
FACES = 4
SUBSTEPS = 2
TERMS = 4
BLOCK = 384
ELEMS = 1024
COMP = 140
TRACE = 60
BND = 128
CP = 144
TP = 64
SLOTS = 4 * BND
CHUNKS = 5
KB = 256

MESH = pl.DeviceIdType.MESH
F32 = jnp.float32
BF16 = jnp.bfloat16
I32 = jnp.int32


def substep_powers():
    one = np.array([1.0 / np.prod(np.arange(1, k + 1)) for k in range(TERMS + 1)])
    total = np.array([1.0])
    for _ in range(SUBSTEPS):
        total = np.convolve(total, one)
    return [float(c) for c in total]


COEF = substep_powers()
DEG = SUBSTEPS * TERMS


def hi_lo(x):
    hi = x.astype(BF16)
    return hi, (x - hi.astype(F32)).astype(BF16)


def right3(x):
    hi, lo = hi_lo(x)
    return jnp.concatenate([hi, hi, lo], axis=0)


def left3(m):
    hi, lo = hi_lo(m)
    return jnp.concatenate([hi, lo, hi], axis=1)


def dot(a, b):
    return jnp.dot(a, b, preferred_element_type=F32)


def one_hot(row, depth):
    n = row.shape[1]
    line = lax.broadcasted_iota(I32, (depth, n), 0)
    return jnp.where(line == jnp.broadcast_to(row, (depth, n)), 1.0, 0.0).astype(BF16)


def look_up(table, index):
    lane = index & 127
    tile = index >> 7
    out = jnp.zeros(index.shape, table.dtype)
    for m in range(table.shape[1] // 128):
        part = jnp.broadcast_to(table[:, 128 * m : 128 * m + 128], index.shape)
        got = jnp.take_along_axis(part, lane, axis=1, mode="promise_in_bounds")
        out = jnp.where(tile == m, got, out)
    return out


def kernel(
    secs,
    rads,
    fields_hbm,
    pattern_hbm,
    order_hbm,
    sizes_hbm,
    neighbours_hbm,
    sends_hbm,
    operator_hbm,
    trace_hbm,
    lift_hbm,
    heights_hbm,
    out,
    fields,
    pattern,
    order,
    sizes,
    neighbours,
    sends,
    operator,
    trace_map,
    lift_map,
    tent_height,
    in_sem,
    xp,
    tp,
    ap,
    lp,
    t3,
    a3,
    l3,
    rows,
    erow,
    ecol,
    scatter,
    pick,
    catch,
    nbx,
    height,
    start_x,
    flow,
    fresh,
    part,
    gath,
    loaded,
    sb,
    rb,
    send_sem,
    recv_sem,
):
    s = lax.axis_index("sector")
    r = lax.axis_index("radial")
    up = lax.rem(s + 1, secs)
    down = lax.rem(s + secs - 1, secs)

    step = COMP * 8 // CHUNKS
    pieces = [pl.ds(step * c, step) for c in range(CHUNKS)]
    loads = [
        pltpu.make_async_copy(src, dst, in_sem.at[i])
        for i, (src, dst) in enumerate(
            [(trace_hbm, trace_map)]
            + [(fields_hbm.at[p], fields.at[p]) for p in pieces]
            + [
                (sends_hbm, sends),
                (operator_hbm, operator),
                (order_hbm, order),
                (sizes_hbm, sizes),
                (neighbours_hbm, neighbours),
                (pattern_hbm, pattern),
                (heights_hbm, tent_height),
                (lift_hbm, lift_map),
            ]
        )
    ]
    for load in loads:
        load.start()

    barrier = pltpu.get_barrier_semaphore()

    def greet(a, b):
        pl.semaphore_signal(barrier, inc=1, device_id=(a, b), device_id_type=MESH)

    greet(up, r)
    greet(down, r)

    @pl.when(r > 0)
    def _():
        greet(s, r - 1)

    @pl.when(r < rads - 1)
    def _():
        greet(s, r + 1)

    @pl.when(r == 0)
    def _():
        rb[:, 2] = jnp.zeros((LEVELS, TP, BND), F32)

    @pl.when(r == rads - 1)
    def _():
        rb[:, 3] = jnp.zeros((LEVELS, TP, BND), F32)

    def copy(level, group, a, b):
        return pltpu.make_async_remote_copy(
            src_ref=sb.at[level, group],
            dst_ref=rb.at[level, group],
            send_sem=send_sem.at[level, group],
            recv_sem=recv_sem.at[level, group],
            device_id=(a, b),
            device_id_type=MESH,
        )

    def start(level):
        @pl.when(r < rads - 1)
        def _():
            copy(level, 2, s, r + 1).start()

        @pl.when(r > 0)
        def _():
            copy(level, 3, s, r - 1).start()

        copy(level, 0, up, r).start()
        copy(level, 1, down, r).start()

    def arrive(level):
        copy(level, 0, up, r).wait_recv()
        copy(level, 1, down, r).wait_recv()

        @pl.when(r > 0)
        def _():
            copy(level, 2, s, r - 1).wait_recv()

        @pl.when(r < rads - 1)
        def _():
            copy(level, 3, s, r + 1).wait_recv()

    def drain(level):
        copy(level, 0, up, r).wait_send()
        copy(level, 1, down, r).wait_send()

        @pl.when(r < rads - 1)
        def _():
            copy(level, 2, s, r + 1).wait_send()

        @pl.when(r > 0)
        def _():
            copy(level, 3, s, r - 1).wait_send()

    def fill_sends(level, got):
        for d in range(4):
            piece = got[:, BND * d : BND * d + BND]
            sb[level, d] = piece[:TP] + piece[TP:]

    tp[...] = jnp.zeros((TP, CP), F32)
    xp[COMP:CP] = jnp.zeros((CP - COMP, ELEMS), F32)
    loads[0].wait()
    tp[0:TRACE, 0:COMP] = trace_map[...]
    t3[0:TP] = left3(tp[...])
    for load in loads[1 : CHUNKS + 1]:
        load.wait()
    for t in range(ELEMS // 128):
        xp[0:COMP, 128 * t : 128 * t + 128] = fields[pl.ds(t, COMP, stride=8)]
    hi, lo = hi_lo(xp[...])
    rows[0:CP] = hi
    rows[CP : 2 * CP] = lo
    first = dot(t3[0:TP], jnp.concatenate([hi, hi, lo], axis=0))
    flow[:, 0:ELEMS] = jnp.concatenate(hi_lo(first), axis=0)
    rest = loads[CHUNKS + 1 :]
    rest[0].wait()
    got = jnp.zeros((2 * TP, SLOTS), F32)
    for m in range(ELEMS // KB):
        got += dot(flow[:, KB * m : KB * m + KB], one_hot(sends[...] - KB * m, KB))
    fill_sends(0, got)
    pl.semaphore_wait(
        barrier, 2 + jnp.where(r > 0, 1, 0) + jnp.where(r < rads - 1, 1, 0)
    )
    start(0)

    ap[...] = jnp.zeros((CP, CP), F32)
    lp[...] = jnp.zeros((FACES * TP, 256), F32)
    rest[1].wait()
    ap[0:COMP, 0:COMP] = operator[...]
    p1 = ap[...]
    a3[0:CP] = left3(p1)
    b1 = right3(p1)
    p2 = dot(a3[0:CP], b1)
    a3[CP : 2 * CP] = left3(p2)
    b2 = right3(p2)
    p34 = dot(a3[0 : 2 * CP], b2)
    a3[2 * CP : 4 * CP] = left3(p34)
    b4 = right3(p34[CP:])
    a3[4 * CP : 8 * CP] = left3(dot(a3[0 : 4 * CP], b4))
    t3[TP : 2 * TP] = left3(dot(t3[0:TP], b1))
    t3[2 * TP : 4 * TP] = left3(dot(t3[0 : 2 * TP], b2))
    t3[4 * TP : 8 * TP] = left3(dot(t3[0 : 4 * TP], b4))
    t3[8 * TP : 9 * TP] = left3(dot(t3[4 * TP : 5 * TP], b4))

    for load in rest[2:7]:
        load.wait()
    line = lax.broadcasted_iota(I32, (16, 128), 0)
    lane = lax.broadcasted_iota(I32, (16, 128), 1)
    shift = jnp.zeros((16, 128), I32)
    limit = jnp.zeros((16, 128), I32)
    begin = jnp.int32(0)
    for l in range(LEVELS):
        size = sizes[l]
        mine = (line >= 3 * l) & (line < 3 * l + 3)
        shift = jnp.where(mine, begin - BLOCK * l, shift)
        limit = jnp.where(mine, BLOCK * l + size, limit)
        begin = begin + size
    slot = 128 * line + lane
    place = jnp.minimum(jnp.maximum(slot + shift, 0), ELEMS - 1)
    element = jnp.where(slot < limit, look_up(order[...], place), -1)
    tall = jnp.concatenate([element.astype(F32), jnp.zeros((112, 128), F32)], axis=0)
    tall = jnp.transpose(tall)
    for l in range(LEVELS):
        for t in range(3):
            n = 3 * l + t
            erow[l, :, 128 * t : 128 * t + 128] = element[n : n + 1]
            ecol[l, 128 * t : 128 * t + 128] = jnp.broadcast_to(tall[:, n : n + 1], (128, 128))
    line = lax.broadcasted_iota(I32, (8, ELEMS), 0)
    extra = jnp.where(line == 0, jnp.broadcast_to(pattern[...], (8, ELEMS)), 0)
    near = neighbours[...]
    numbers = jnp.concatenate([near >> 8, near & 255, extra], axis=0)
    rows[2 * CP :] = numbers.astype(F32).astype(BF16)
    rest[7].wait()
    for f in range(FACES):
        lp[TP * f : TP * f + TRACE, 0:COMP] = lift_map[:, f]
    l3[...] = left3(jnp.transpose(lp[...])[0:CP])
    out[...] = jnp.zeros((COMP * 8, 128), F32)

    def weights(l):
        h = height[l]
        power = jnp.ones_like(h)
        ws = []
        for k in range(1, DEG + 1):
            power = power * h
            ws.append(power * COEF[k])
        return ws

    def finish(l):
        x = loaded[...]
        x3 = right3(x)
        y = x
        ws = weights(l)
        for k in range(1, DEG + 1):
            y += dot(a3[CP * (k - 1) : CP * k], x3) * ws[k - 1]
        hl = jnp.concatenate(hi_lo(y), axis=0)
        for n in range(ELEMS // KB):
            here = slice(KB * n, KB * n + KB)
            got = dot(hl, scatter[:, here])
            got = got[:COMP] + got[CP : CP + COMP]
            for t in range(KB // 128):
                place = pl.ds(n * (KB // 128) + t, COMP, stride=8)
                out[place] += got[:, 128 * t : 128 * t + 128]

    def level(l, carry):
        @pl.when(l > 0)
        def _():
            finish(l - 1)
            for n in range(ELEMS // KB):
                here = slice(KB * n, KB * n + KB)
                flow[:, here] += dot(fresh[...], scatter[:, here]).astype(BF16)

        moved = jnp.zeros((2 * CP + 16, BLOCK), F32)
        for m in range(ELEMS // KB):
            moved += dot(rows[:, KB * m : KB * m + KB], one_hot(erow[l] - KB * m, KB))
        start_x[...] = moved[:CP] + moved[CP : 2 * CP]
        numbers = moved[2 * CP :].astype(I32)
        nbx[...] = numbers[0:4] * 256 + numbers[4:8]
        kind = numbers[8:9]
        h = jnp.zeros((1, BLOCK), F32)
        for p in range(16):
            h = jnp.where(kind == p, tent_height[p], h)
        height[l] = h
        for f in range(FACES):
            row = nbx[f : f + 1]
            acc = jnp.zeros((2 * TP, BLOCK), F32)
            for m in range(ELEMS // KB):
                acc += dot(flow[:, KB * m : KB * m + KB], one_hot(row - KB * m, KB))
            gath[f] = acc
            catch[:, BLOCK * f : BLOCK * f + BLOCK] = one_hot(row - ELEMS, SLOTS)
        for t in range(ELEMS // 128):
            row = lax.broadcasted_iota(I32, (BLOCK, 128), 1).astype(F32) + 128.0 * t
            hit = jnp.where(ecol[l] == row, 1.0, 0.0).astype(BF16)
            scatter[:, 128 * t : 128 * t + 128] = hit

        @pl.when(l < LEVELS - 1)
        def _():
            gone = dot(jnp.ones((16, BLOCK), BF16), scatter[...])[0:1]
            keep = jnp.broadcast_to(1.0 - gone, (2 * TP, ELEMS))
            flow[:, 0:ELEMS] = (flow[:, 0:ELEMS].astype(F32) * keep).astype(BF16)
            got = jnp.zeros((2 * TP, SLOTS), F32)
            for m in range(ELEMS // KB):
                got += dot(flow[:, KB * m : KB * m + KB], one_hot(sends[...] - KB * m, KB))
            part[...] = got
            for d in range(4):
                row = sends[:, BND * d : BND * d + BND].astype(F32)
                hit = jnp.where(ecol[l] == jnp.broadcast_to(row, (BLOCK, BND)), 1.0, 0.0)
                pick[:, BND * d : BND * d + BND] = hit.astype(BF16)

        arrive(l)
        come = jnp.concatenate([rb[l, d] for d in range(4)], axis=1)
        come = dot(jnp.concatenate(hi_lo(come), axis=0), catch[...])
        his, los = [], []
        for f in range(FACES):
            acc = (gath[f] + come[:, BLOCK * f : BLOCK * f + BLOCK]).astype(BF16)
            his.append(acc[:TP])
            los.append(acc[TP:])
        x = start_x[...] + dot(l3[...], jnp.concatenate(his + his + los, axis=0))
        loaded[...] = x

        @pl.when(l < LEVELS - 1)
        def _():
            x3 = right3(x)
            ws = weights(l)
            o = dot(t3[0:TP], x3)
            for k in range(1, DEG + 1):
                o += dot(t3[TP * k : TP * k + TP], x3) * ws[k - 1]
            o = jnp.concatenate(hi_lo(o), axis=0)
            fresh[...] = o
            fill_sends(l + 1, part[...] + dot(o, pick[...]))
            start(l + 1)

        return carry

    lax.fori_loop(0, LEVELS, level, 0)
    finish(LEVELS - 1)
    for l in range(LEVELS):
        drain(l)


def solution(mesh):
    secs, rads = mesh.shape["sector"], mesh.shape["radial"]
    hbm = pl.BlockSpec(memory_space=pltpu.HBM)

    def body(
        fields,
        pattern,
        tent_order,
        level_sizes,
        send_rows,
        neighbours,
        operator,
        trace_map,
        lift_map,
        tent_height,
    ):
        args = (
            fields.reshape(COMP * 8, 128),
            pattern[0],
            tent_order[0],
            level_sizes[0, 0],
            neighbours[0, 0],
            send_rows.reshape(1, SLOTS),
            operator,
            trace_map,
            jnp.transpose(lift_map, (2, 0, 1)),
            tent_height,
        )
        args = tuple(pltpu.with_memory_space_constraint(a, pltpu.HBM) for a in args)
        homes = [
            (pltpu.SMEM if len(a.shape) == 1 else pltpu.VMEM)(a.shape, a.dtype) for a in args
        ]
        out = pl.pallas_call(
            functools.partial(kernel, secs, rads),
            out_shape=jax.ShapeDtypeStruct((COMP * 8, 128), F32),
            in_specs=[hbm] * len(args),
            out_specs=pl.BlockSpec(memory_space=pltpu.VMEM),
            scratch_shapes=homes
            + [
                pltpu.SemaphoreType.DMA((len(args) - 1 + CHUNKS,)),
                pltpu.VMEM((CP, ELEMS), F32),
                pltpu.VMEM((TP, CP), F32),
                pltpu.VMEM((CP, CP), F32),
                pltpu.VMEM((FACES * TP, 256), F32),
                pltpu.VMEM(((DEG + 1) * TP, 3 * CP), BF16),
                pltpu.VMEM((DEG * CP, 3 * CP), BF16),
                pltpu.VMEM((CP, 3 * FACES * TP), BF16),
                pltpu.VMEM((2 * CP + 16, ELEMS), BF16),
                pltpu.VMEM((LEVELS, 1, BLOCK), I32),
                pltpu.VMEM((LEVELS, BLOCK, 128), F32),
                pltpu.VMEM((BLOCK, ELEMS), BF16),
                pltpu.VMEM((BLOCK, SLOTS), BF16),
                pltpu.VMEM((SLOTS, FACES * BLOCK), BF16),
                pltpu.VMEM((FACES, BLOCK), I32),
                pltpu.VMEM((LEVELS, 1, BLOCK), F32),
                pltpu.VMEM((CP, BLOCK), F32),
                pltpu.VMEM((2 * TP, ELEMS), BF16),
                pltpu.VMEM((2 * TP, BLOCK), BF16),
                pltpu.VMEM((2 * TP, SLOTS), F32),
                pltpu.VMEM((FACES, 2 * TP, BLOCK), F32),
                pltpu.VMEM((CP, BLOCK), F32),
                pltpu.VMEM((LEVELS, 4, TP, BND), F32),
                pltpu.VMEM((LEVELS, 4, TP, BND), F32),
                pltpu.SemaphoreType.DMA((LEVELS, 4)),
                pltpu.SemaphoreType.DMA((LEVELS, 4)),
            ],
            compiler_params=pltpu.CompilerParams(
                collective_id=0, has_side_effects=True, vmem_limit_bytes=32 * 2**20
            ),
            name="tent_layer",
        )(*args)
        return out.reshape(1, 1, COMP, ELEMS)

    block = P("sector", "radial", None)
    wide = P("sector", "radial", None, None)
    return jax.shard_map(
        body,
        mesh=mesh,
        in_specs=(wide, block, block, block, wide, wide, P(), P(), P(), P()),
        out_specs=wide,
        check_vma=False,
    )
```

time: 47.5 us -> 37.1 us (0.78)
  local copies, waits for them, and re-layouts: 6.28 us -> 0.81 us
  Pallas kernels: 41 us -> 36.1 us
    pallas_call x1, Pallas kernels: 41 us -> 36.1 us  [body(): pl.pallas_call(functools.partial(kernel, secs, rads), out_shape=jax.Shape...]
    unnamed x2 -> x1, local copies, waits for them, and re-layouts: 3.81 us -> 0.81 us
    broadcast_in_dim x1 -> x0, local copies, waits for them, and re-layouts: 2.46 us -> none  [body(): return out[None, None]]
where the time goes in v1:
time: 37.1 us; the launch traced here: 36.9 us
  Pallas kernels  36.1 us (97%)
  local copies, waits for them, and re-layouts  0.81 us (2%)
    pallas_call x1, Pallas kernels, body(): pl.pallas_call(functools.partial(kernel, secs, rads), out_shape=jax.Shape...  36.1 us
    unnamed x1, local copies, waits for them, and re-layouts  0.81 us

profile of v1, /device:TPU:2, one launch (start us, length us, event | category | flops | bytes accessed | tf_op | source)
XLA Modules:
  0.0 36.9 jit_solution(2730157034627476890)
XLA Ops:
  0.0 36.1 %tent_layer.1 = f32[1120,128]{1,0:T(8,128)S(1)} custom-call(f32[1120,128]{1,0:T(8,128)} %bitcast.9, s32[1,1024]{1,0:T(1,128)} %bitcast.12, s32[1,1024]{1,0:T(1,128)} %bitcast.13, s32[4]{0:T(128)} %bitcast.15, s32[4,1024]{1,0:T(4,128)} %bitcast.11, s32[1,512]{1,0:T(1,128)} %bitcast.14, f32[140,140]{1,0:T(8,128)} %operator_hbm.1, f32[60,140]{1,0:T(8,128)} %trace_hbm.1, ...), custom_call_target="tpu_custom_call" | custom-call | tf_op jit(solution)/shard_map/tent_layer/pallas_call | solution.py:444
  36.1 0.8 %copy.14 = f32[1,1,140,1024]{3,1,2,0:T(1,128)} copy(f32[1,1,140,1024]{3,1,2,0:T(1,128)S(1)} %bitcast.8) | data formatting | bytes 1146880

commit v2 on v1

--- a/solution.py
+++ b/solution.py
@@ -20,7 +20,7 @@
 CP = 144
 TP = 64
 SLOTS = 4 * BND
-CHUNKS = 5
+TILES = ELEMS // 128
 KB = 256
 
 MESH = pl.DeviceIdType.MESH
@@ -39,6 +39,7 @@
 
 COEF = substep_powers()
 DEG = SUBSTEPS * TERMS
+HALF = DEG // 2
 
 
 def hi_lo(x):
@@ -60,10 +61,11 @@
     return jnp.dot(a, b, preferred_element_type=F32)
 
 
-def one_hot(row, depth):
+def one_hot(row, base):
     n = row.shape[1]
-    line = lax.broadcasted_iota(I32, (depth, n), 0)
-    return jnp.where(line == jnp.broadcast_to(row, (depth, n)), 1.0, 0.0).astype(BF16)
+    line = lax.broadcasted_iota(I32, (KB, n), 0).astype(F32).astype(BF16)
+    row = jnp.minimum(jnp.maximum(row - base, -1), KB).astype(F32).astype(BF16)
+    return jnp.where(line == jnp.broadcast_to(row, (KB, n)), jnp.bfloat16(1), jnp.bfloat16(0))
 
 
 def look_up(table, index):
@@ -102,7 +104,6 @@
     lift_map,
     tent_height,
     in_sem,
-    xp,
     tp,
     ap,
     lp,
@@ -114,6 +115,7 @@
     ecol,
     scatter,
     pick,
+    listed,
     catch,
     nbx,
     height,
@@ -133,27 +135,36 @@
     up = lax.rem(s + 1, secs)
     down = lax.rem(s + secs - 1, secs)
 
-    step = COMP * 8 // CHUNKS
-    pieces = [pl.ds(step * c, step) for c in range(CHUNKS)]
-    loads = [
-        pltpu.make_async_copy(src, dst, in_sem.at[i])
-        for i, (src, dst) in enumerate(
-            [(trace_hbm, trace_map)]
-            + [(fields_hbm.at[p], fields.at[p]) for p in pieces]
-            + [
-                (sends_hbm, sends),
-                (operator_hbm, operator),
-                (order_hbm, order),
-                (sizes_hbm, sizes),
-                (neighbours_hbm, neighbours),
-                (pattern_hbm, pattern),
-                (heights_hbm, tent_height),
-                (lift_hbm, lift_map),
+    loads = {
+        name: pltpu.make_async_copy(src, dst, in_sem.at[i])
+        for i, (name, src, dst) in enumerate(
+            [
+                ("sends", sends_hbm, sends),
+                ("trace", trace_hbm, trace_map),
+                *((t, fields_hbm.at[:, t], fields.at[t, pl.ds(0, COMP)]) for t in range(TILES)),
+                ("operator", operator_hbm, operator),
+                ("order", order_hbm, order),
+                ("sizes", sizes_hbm, sizes),
+                ("neighbours", neighbours_hbm, neighbours),
+                ("pattern", pattern_hbm, pattern),
+                ("heights", heights_hbm, tent_height),
+                ("lift", lift_hbm, lift_map),
             ]
         )
-    ]
-    for load in loads:
-        load.start()
+    }
+    urgent = ("sends", "trace", *range(TILES))
+    for name in urgent:
+        loads[name].start()
+
+    rb[:, :, TRACE:TP] = jnp.zeros((LEVELS, 4, TP - TRACE, BND), F32)
+
+    @pl.when(r == 0)
+    def _():
+        rb[:, 2] = jnp.zeros((LEVELS, TP, BND), F32)
+
+    @pl.when(r == rads - 1)
+    def _():
+        rb[:, 3] = jnp.zeros((LEVELS, TP, BND), F32)
 
     barrier = pltpu.get_barrier_semaphore()
 
@@ -171,18 +182,14 @@
     def _():
         greet(s, r + 1)
 
-    @pl.when(r == 0)
-    def _():
-        rb[:, 2] = jnp.zeros((LEVELS, TP, BND), F32)
-
-    @pl.when(r == rads - 1)
-    def _():
-        rb[:, 3] = jnp.zeros((LEVELS, TP, BND), F32)
+    for name in loads:
+        if name not in urgent:
+            loads[name].start()
 
     def copy(level, group, a, b):
         return pltpu.make_async_remote_copy(
-            src_ref=sb.at[level, group],
-            dst_ref=rb.at[level, group],
+            src_ref=sb.at[level, group, pl.ds(0, TRACE)],
+            dst_ref=rb.at[level, group, pl.ds(0, TRACE)],
             send_sem=send_sem.at[level, group],
             recv_sem=recv_sem.at[level, group],
             device_id=(a, b),
@@ -231,33 +238,31 @@
             sb[level, d] = piece[:TP] + piece[TP:]
 
     tp[...] = jnp.zeros((TP, CP), F32)
-    xp[COMP:CP] = jnp.zeros((CP - COMP, ELEMS), F32)
-    loads[0].wait()
+    fields[:, COMP:CP] = jnp.zeros((TILES, CP - COMP, 128), F32)
+    loads["sends"].wait()
+    for m in range(ELEMS // KB):
+        listed[KB * m : KB * m + KB] = one_hot(sends[...], KB * m)
+    loads["trace"].wait()
     tp[0:TRACE, 0:COMP] = trace_map[...]
     t3[0:TP] = left3(tp[...])
-    for load in loads[1 : CHUNKS + 1]:
-        load.wait()
-    for t in range(ELEMS // 128):
-        xp[0:COMP, 128 * t : 128 * t + 128] = fields[pl.ds(t, COMP, stride=8)]
-    hi, lo = hi_lo(xp[...])
-    rows[0:CP] = hi
-    rows[CP : 2 * CP] = lo
-    first = dot(t3[0:TP], jnp.concatenate([hi, hi, lo], axis=0))
-    flow[:, 0:ELEMS] = jnp.concatenate(hi_lo(first), axis=0)
-    rest = loads[CHUNKS + 1 :]
-    rest[0].wait()
-    got = jnp.zeros((2 * TP, SLOTS), F32)
-    for m in range(ELEMS // KB):
-        got += dot(flow[:, KB * m : KB * m + KB], one_hot(sends[...] - KB * m, KB))
+    for t in range(TILES):
+        loads[t].wait()
+    hi, lo = hi_lo(jnp.concatenate([fields[t] for t in range(TILES)], axis=1))
+    o = dot(t3[0:TP], jnp.concatenate([hi, hi, lo], axis=0))
+    o = jnp.concatenate(hi_lo(o), axis=0)
+    got = dot(o, listed[...])
     fill_sends(0, got)
     pl.semaphore_wait(
         barrier, 2 + jnp.where(r > 0, 1, 0) + jnp.where(r < rads - 1, 1, 0)
     )
     start(0)
+    flow[...] = o
+    rows[0:CP] = hi
+    rows[CP : 2 * CP] = lo
 
     ap[...] = jnp.zeros((CP, CP), F32)
     lp[...] = jnp.zeros((FACES * TP, 256), F32)
-    rest[1].wait()
+    loads["operator"].wait()
     ap[0:COMP, 0:COMP] = operator[...]
     p1 = ap[...]
     a3[0:CP] = left3(p1)
@@ -268,14 +273,13 @@
     p34 = dot(a3[0 : 2 * CP], b2)
     a3[2 * CP : 4 * CP] = left3(p34)
     b4 = right3(p34[CP:])
-    a3[4 * CP : 8 * CP] = left3(dot(a3[0 : 4 * CP], b4))
     t3[TP : 2 * TP] = left3(dot(t3[0:TP], b1))
     t3[2 * TP : 4 * TP] = left3(dot(t3[0 : 2 * TP], b2))
     t3[4 * TP : 8 * TP] = left3(dot(t3[0 : 4 * TP], b4))
     t3[8 * TP : 9 * TP] = left3(dot(t3[4 * TP : 5 * TP], b4))
 
-    for load in rest[2:7]:
-        load.wait()
+    for name in ("order", "sizes", "neighbours", "pattern", "heights"):
+        loads[name].wait()
     line = lax.broadcasted_iota(I32, (16, 128), 0)
     lane = lax.broadcasted_iota(I32, (16, 128), 1)
     shift = jnp.zeros((16, 128), I32)
@@ -302,28 +306,29 @@
     near = neighbours[...]
     numbers = jnp.concatenate([near >> 8, near & 255, extra], axis=0)
     rows[2 * CP :] = numbers.astype(F32).astype(BF16)
-    rest[7].wait()
+    loads["lift"].wait()
     for f in range(FACES):
         lp[TP * f : TP * f + TRACE, 0:COMP] = lift_map[:, f]
     l3[...] = left3(jnp.transpose(lp[...])[0:CP])
-    out[...] = jnp.zeros((COMP * 8, 128), F32)
-
-    def weights(l):
+
+    def powers(l):
         h = height[l]
-        power = jnp.ones_like(h)
-        ws = []
-        for k in range(1, DEG + 1):
-            power = power * h
-            ws.append(power * COEF[k])
-        return ws
+        ps = [jnp.ones_like(h)]
+        for k in range(DEG):
+            ps.append(ps[k] * h)
+        return ps
 
     def finish(l):
         x = loaded[...]
         x3 = right3(x)
-        y = x
-        ws = weights(l)
-        for k in range(1, DEG + 1):
-            y += dot(a3[CP * (k - 1) : CP * k], x3) * ws[k - 1]
+        hs = powers(l)
+        y, v = x, x * COEF[HALF]
+        for k in range(1, HALF + 1):
+            u = dot(a3[CP * (k - 1) : CP * k], x3)
+            if k < HALF:
+                y += u * (hs[k] * COEF[k])
+            v += u * (hs[k] * COEF[HALF + k])
+        y += dot(a3[CP * (HALF - 1) :], right3(v * hs[HALF]))
         hl = jnp.concatenate(hi_lo(y), axis=0)
         for n in range(ELEMS // KB):
             here = slice(KB * n, KB * n + KB)
@@ -331,83 +336,79 @@
             got = got[:COMP] + got[CP : CP + COMP]
             for t in range(KB // 128):
                 place = pl.ds(n * (KB // 128) + t, COMP, stride=8)
-                out[place] += got[:, 128 * t : 128 * t + 128]
-
-    def level(l, carry):
-        @pl.when(l > 0)
-        def _():
+                if l == 0:
+                    out[place] = got[:, 128 * t : 128 * t + 128]
+                else:
+                    out[place] += got[:, 128 * t : 128 * t + 128]
+
+    for l in range(LEVELS):
+        if l > 0:
             finish(l - 1)
+            ones = jnp.ones((16, BLOCK), BF16)
             for n in range(ELEMS // KB):
                 here = slice(KB * n, KB * n + KB)
-                flow[:, here] += dot(fresh[...], scatter[:, here]).astype(BF16)
+                got = dot(jnp.concatenate([fresh[...], ones], axis=0), scatter[:, here])
+                keep = jnp.broadcast_to(1.0 - got[2 * TP : 2 * TP + 1], (2 * TP, KB))
+                flow[:, here] = (flow[:, here].astype(F32) * keep + got[: 2 * TP]).astype(BF16)
 
         moved = jnp.zeros((2 * CP + 16, BLOCK), F32)
         for m in range(ELEMS // KB):
-            moved += dot(rows[:, KB * m : KB * m + KB], one_hot(erow[l] - KB * m, KB))
+            moved += dot(rows[:, KB * m : KB * m + KB], one_hot(erow[l], KB * m))
         start_x[...] = moved[:CP] + moved[CP : 2 * CP]
         numbers = moved[2 * CP :].astype(I32)
-        nbx[...] = numbers[0:4] * 256 + numbers[4:8]
+        near = numbers[0:4] * 256 + numbers[4:8]
+        for f in range(FACES):
+            nbx[:, BLOCK * f : BLOCK * f + BLOCK] = near[f : f + 1]
         kind = numbers[8:9]
         h = jnp.zeros((1, BLOCK), F32)
         for p in range(16):
             h = jnp.where(kind == p, tent_height[p], h)
         height[l] = h
-        for f in range(FACES):
-            row = nbx[f : f + 1]
-            acc = jnp.zeros((2 * TP, BLOCK), F32)
+        for f in range(0, FACES * BLOCK, 2 * KB):
+            here = slice(f, f + 2 * KB)
+            row = nbx[:, here]
+            acc = jnp.zeros((2 * TP, 2 * KB), F32)
             for m in range(ELEMS // KB):
-                acc += dot(flow[:, KB * m : KB * m + KB], one_hot(row - KB * m, KB))
-            gath[f] = acc
-            catch[:, BLOCK * f : BLOCK * f + BLOCK] = one_hot(row - ELEMS, SLOTS)
+                acc += dot(flow[:, KB * m : KB * m + KB], one_hot(row, KB * m))
+            gath[:, here] = acc
+            for m in range(SLOTS // KB):
+                catch[KB * m : KB * m + KB, here] = one_hot(row, ELEMS + KB * m)
         for t in range(ELEMS // 128):
             row = lax.broadcasted_iota(I32, (BLOCK, 128), 1).astype(F32) + 128.0 * t
             hit = jnp.where(ecol[l] == row, 1.0, 0.0).astype(BF16)
             scatter[:, 128 * t : 128 * t + 128] = hit
-
-        @pl.when(l < LEVELS - 1)
-        def _():
-            gone = dot(jnp.ones((16, BLOCK), BF16), scatter[...])[0:1]
-            keep = jnp.broadcast_to(1.0 - gone, (2 * TP, ELEMS))
-            flow[:, 0:ELEMS] = (flow[:, 0:ELEMS].astype(F32) * keep).astype(BF16)
-            got = jnp.zeros((2 * TP, SLOTS), F32)
-            for m in range(ELEMS // KB):
-                got += dot(flow[:, KB * m : KB * m + KB], one_hot(sends[...] - KB * m, KB))
-            part[...] = got
+        if l < LEVELS - 1:
+            got = dot(flow[...], listed[...])
             for d in range(4):
                 row = sends[:, BND * d : BND * d + BND].astype(F32)
                 hit = jnp.where(ecol[l] == jnp.broadcast_to(row, (BLOCK, BND)), 1.0, 0.0)
                 pick[:, BND * d : BND * d + BND] = hit.astype(BF16)
-
+            gone = dot(jnp.ones((16, BLOCK), BF16), pick[...])[0:1]
+            part[...] = got * jnp.broadcast_to(1.0 - gone, (2 * TP, SLOTS))
+        drain(l)
         arrive(l)
         come = jnp.concatenate([rb[l, d] for d in range(4)], axis=1)
         come = dot(jnp.concatenate(hi_lo(come), axis=0), catch[...])
         his, los = [], []
         for f in range(FACES):
-            acc = (gath[f] + come[:, BLOCK * f : BLOCK * f + BLOCK]).astype(BF16)
+            here = slice(BLOCK * f, BLOCK * f + BLOCK)
+            acc = (gath[:, here] + come[:, here]).astype(BF16)
             his.append(acc[:TP])
             los.append(acc[TP:])
         x = start_x[...] + dot(l3[...], jnp.concatenate(his + his + los, axis=0))
         loaded[...] = x
-
-        @pl.when(l < LEVELS - 1)
-        def _():
+        if l < LEVELS - 1:
             x3 = right3(x)
-            ws = weights(l)
+            hs = powers(l)
             o = dot(t3[0:TP], x3)
             for k in range(1, DEG + 1):
-                o += dot(t3[TP * k : TP * k + TP], x3) * ws[k - 1]
+                o += dot(t3[TP * k : TP * k + TP], x3) * (hs[k] * COEF[k])
             o = jnp.concatenate(hi_lo(o), axis=0)
             fresh[...] = o
             fill_sends(l + 1, part[...] + dot(o, pick[...]))
             start(l + 1)
 
-        return carry
-
-    lax.fori_loop(0, LEVELS, level, 0)
     finish(LEVELS - 1)
-    for l in range(LEVELS):
-        drain(l)
-
 
 def solution(mesh):
     secs, rads = mesh.shape["sector"], mesh.shape["radial"]
@@ -426,7 +427,7 @@
         tent_height,
     ):
         args = (
-            fields.reshape(COMP * 8, 128),
+            fields.reshape(COMP, TILES, 128),
             pattern[0],
             tent_order[0],
             level_sizes[0, 0],
@@ -438,8 +439,8 @@
             tent_height,
         )
         args = tuple(pltpu.with_memory_space_constraint(a, pltpu.HBM) for a in args)
-        homes = [
-            (pltpu.SMEM if len(a.shape) == 1 else pltpu.VMEM)(a.shape, a.dtype) for a in args
+        homes = [pltpu.VMEM((TILES, CP, 128), F32)] + [
+            (pltpu.SMEM if len(a.shape) == 1 else pltpu.VMEM)(a.shape, a.dtype) for a in args[1:]
         ]
         out = pl.pallas_call(
             functools.partial(kernel, secs, rads),
@@ -448,27 +449,27 @@
             out_specs=pl.BlockSpec(memory_space=pltpu.VMEM),
             scratch_shapes=homes
             + [
-                pltpu.SemaphoreType.DMA((len(args) - 1 + CHUNKS,)),
-                pltpu.VMEM((CP, ELEMS), F32),
+                pltpu.SemaphoreType.DMA((TILES + len(args) - 1,)),
                 pltpu.VMEM((TP, CP), F32),
                 pltpu.VMEM((CP, CP), F32),
                 pltpu.VMEM((FACES * TP, 256), F32),
                 pltpu.VMEM(((DEG + 1) * TP, 3 * CP), BF16),
-                pltpu.VMEM((DEG * CP, 3 * CP), BF16),
+                pltpu.VMEM((HALF * CP, 3 * CP), BF16),
                 pltpu.VMEM((CP, 3 * FACES * TP), BF16),
                 pltpu.VMEM((2 * CP + 16, ELEMS), BF16),
                 pltpu.VMEM((LEVELS, 1, BLOCK), I32),
                 pltpu.VMEM((LEVELS, BLOCK, 128), F32),
                 pltpu.VMEM((BLOCK, ELEMS), BF16),
                 pltpu.VMEM((BLOCK, SLOTS), BF16),
+                pltpu.VMEM((ELEMS, SLOTS), BF16),
                 pltpu.VMEM((SLOTS, FACES * BLOCK), BF16),
-                pltpu.VMEM((FACES, BLOCK), I32),
+                pltpu.VMEM((1, FACES * BLOCK), I32),
                 pltpu.VMEM((LEVELS, 1, BLOCK), F32),
                 pltpu.VMEM((CP, BLOCK), F32),
                 pltpu.VMEM((2 * TP, ELEMS), BF16),
                 pltpu.VMEM((2 * TP, BLOCK), BF16),
                 pltpu.VMEM((2 * TP, SLOTS), F32),
-                pltpu.VMEM((FACES, 2 * TP, BLOCK), F32),
+                pltpu.VMEM((2 * TP, FACES * BLOCK), F32),
                 pltpu.VMEM((CP, BLOCK), F32),
                 pltpu.VMEM((LEVELS, 4, TP, BND), F32),
                 pltpu.VMEM((LEVELS, 4, TP, BND), F32),

time: 37.1 us -> 35.3 us (0.951)
  Pallas kernels: 36.1 us -> 34.3 us
    pallas_call x1, Pallas kernels: 36.1 us -> 34.3 us  [body(): pl.pallas_call(functools.partial(kernel, secs, rads), out_shape=jax.Shape...]
where the time goes in v2:
time: 35.3 us; the launch traced here: 35.1 us
  Pallas kernels  34.3 us (97%)
  local copies, waits for them, and re-layouts  0.81 us (2%)
    pallas_call x1, Pallas kernels, body(): pl.pallas_call(functools.partial(kernel, secs, rads), out_shape=jax.Shape...  34.3 us
    unnamed x1, local copies, waits for them, and re-layouts  0.81 us

profile of v2, /device:TPU:2, one launch (start us, length us, event | category | flops | bytes accessed | tf_op | source)
XLA Modules:
  0.0 35.1 jit_solution(12737425146288142344)
XLA Ops:
  0.0 34.3 %tent_layer.1 = f32[1120,128]{1,0:T(8,128)S(1)} custom-call(f32[140,8,128]{2,1,0:T(8,128)} %bitcast.9, s32[1,1024]{1,0:T(1,128)} %bitcast.12, s32[1,1024]{1,0:T(1,128)} %bitcast.13, s32[4]{0:T(128)} %bitcast.15, s32[4,1024]{1,0:T(4,128)} %bitcast.11, s32[1,512]{1,0:T(1,128)} %bitcast.14, f32[140,140]{1,0:T(8,128)} %operator_hbm.1, f32[60,140]{1,0:T(8,128)} %trace_hbm.1, ...), custom_call_target="tpu_custom_call" | custom-call | tf_op jit(solution)/shard_map/tent_layer/pallas_call | solution.py:445
  34.3 0.8 %copy.14 = f32[1,1,140,1024]{3,1,2,0:T(1,128)} copy(f32[1,1,140,1024]{3,1,2,0:T(1,128)S(1)} %bitcast.8) | data formatting | bytes 1146880

commit v3 on v2

--- a/solution.py
+++ b/solution.py
@@ -141,7 +141,7 @@
             [
                 ("sends", sends_hbm, sends),
                 ("trace", trace_hbm, trace_map),
-                *((t, fields_hbm.at[:, t], fields.at[t, pl.ds(0, COMP)]) for t in range(TILES)),
+                ("fields", fields_hbm, fields),
                 ("operator", operator_hbm, operator),
                 ("order", order_hbm, order),
                 ("sizes", sizes_hbm, sizes),
@@ -152,7 +152,7 @@
             ]
         )
     }
-    urgent = ("sends", "trace", *range(TILES))
+    urgent = ("fields", "sends", "trace")
     for name in urgent:
         loads[name].start()
 
@@ -190,8 +190,8 @@
         return pltpu.make_async_remote_copy(
             src_ref=sb.at[level, group, pl.ds(0, TRACE)],
             dst_ref=rb.at[level, group, pl.ds(0, TRACE)],
-            send_sem=send_sem.at[level, group],
-            recv_sem=recv_sem.at[level, group],
+            send_sem=send_sem.at[level % 2, group],
+            recv_sem=recv_sem.at[level % 2, group],
             device_id=(a, b),
             device_id_type=MESH,
         )
@@ -238,16 +238,17 @@
             sb[level, d] = piece[:TP] + piece[TP:]
 
     tp[...] = jnp.zeros((TP, CP), F32)
-    fields[:, COMP:CP] = jnp.zeros((TILES, CP - COMP, 128), F32)
     loads["sends"].wait()
     for m in range(ELEMS // KB):
         listed[KB * m : KB * m + KB] = one_hot(sends[...], KB * m)
     loads["trace"].wait()
     tp[0:TRACE, 0:COMP] = trace_map[...]
     t3[0:TP] = left3(tp[...])
-    for t in range(TILES):
-        loads[t].wait()
-    hi, lo = hi_lo(jnp.concatenate([fields[t] for t in range(TILES)], axis=1))
+    loads["fields"].wait()
+    piece = [fields[pl.ds(t, COMP, stride=TILES)] for t in range(TILES)]
+    piece = jnp.concatenate(piece, axis=1)
+    piece = jnp.concatenate([piece, jnp.zeros((CP - COMP, ELEMS), F32)], axis=0)
+    hi, lo = hi_lo(piece)
     o = dot(t3[0:TP], jnp.concatenate([hi, hi, lo], axis=0))
     o = jnp.concatenate(hi_lo(o), axis=0)
     got = dot(o, listed[...])
@@ -427,7 +428,7 @@
         tent_height,
     ):
         args = (
-            fields.reshape(COMP, TILES, 128),
+            fields.reshape(COMP * TILES, 128),
             pattern[0],
             tent_order[0],
             level_sizes[0, 0],
@@ -439,8 +440,8 @@
             tent_height,
         )
         args = tuple(pltpu.with_memory_space_constraint(a, pltpu.HBM) for a in args)
-        homes = [pltpu.VMEM((TILES, CP, 128), F32)] + [
-            (pltpu.SMEM if len(a.shape) == 1 else pltpu.VMEM)(a.shape, a.dtype) for a in args[1:]
+        homes = [
+            (pltpu.SMEM if len(a.shape) == 1 else pltpu.VMEM)(a.shape, a.dtype) for a in args
         ]
         out = pl.pallas_call(
             functools.partial(kernel, secs, rads),
@@ -449,7 +450,7 @@
             out_specs=pl.BlockSpec(memory_space=pltpu.VMEM),
             scratch_shapes=homes
             + [
-                pltpu.SemaphoreType.DMA((TILES + len(args) - 1,)),
+                pltpu.SemaphoreType.DMA((len(args),)),
                 pltpu.VMEM((TP, CP), F32),
                 pltpu.VMEM((CP, CP), F32),
                 pltpu.VMEM((FACES * TP, 256), F32),
@@ -473,8 +474,8 @@
                 pltpu.VMEM((CP, BLOCK), F32),
                 pltpu.VMEM((LEVELS, 4, TP, BND), F32),
                 pltpu.VMEM((LEVELS, 4, TP, BND), F32),
-                pltpu.SemaphoreType.DMA((LEVELS, 4)),
-                pltpu.SemaphoreType.DMA((LEVELS, 4)),
+                pltpu.SemaphoreType.DMA((2, 4)),
+                pltpu.SemaphoreType.DMA((2, 4)),
             ],
             compiler_params=pltpu.CompilerParams(
                 collective_id=0, has_side_effects=True, vmem_limit_bytes=32 * 2**20

time: 35.3 us -> 35.1 us (level)
  no operation moved by 1% of the time
where the time goes in v3:
time: 35.1 us; the launch traced here: 34.9 us
  Pallas kernels  34.1 us (97%)
  local copies, waits for them, and re-layouts  0.81 us (2%)
    pallas_call x1, Pallas kernels, body(): pl.pallas_call(functools.partial(kernel, secs, rads), out_shape=jax.Shape...  34.1 us
    unnamed x1, local copies, waits for them, and re-layouts  0.81 us

profile of v3, /device:TPU:2, one launch (start us, length us, event | category | flops | bytes accessed | tf_op | source)
XLA Modules:
  0.0 34.9 jit_solution(3105902721622479783)
XLA Ops:
  0.0 34.1 %tent_layer.1 = f32[1120,128]{1,0:T(8,128)S(1)} custom-call(f32[1120,128]{1,0:T(8,128)} %bitcast.9, s32[1,1024]{1,0:T(1,128)} %bitcast.12, s32[1,1024]{1,0:T(1,128)} %bitcast.13, s32[4]{0:T(128)} %bitcast.15, s32[4,1024]{1,0:T(4,128)} %bitcast.11, s32[1,512]{1,0:T(1,128)} %bitcast.14, f32[140,140]{1,0:T(8,128)} %operator_hbm.1, f32[60,140]{1,0:T(8,128)} %trace_hbm.1, ...), custom_call_target="tpu_custom_call" | custom-call | tf_op jit(solution)/shard_map/tent_layer/pallas_call | solution.py:446
  34.1 0.8 %copy.14 = f32[1,1,140,1024]{3,1,2,0:T(1,128)} copy(f32[1,1,140,1024]{3,1,2,0:T(1,128)S(1)} %bitcast.8) | data formatting | bytes 1146880

commit v4 on v3

--- a/solution.py
+++ b/solution.py
@@ -112,14 +112,15 @@
     l3,
     rows,
     erow,
-    ecol,
+    ehi,
+    elo,
     scatter,
+    ends,
     pick,
     listed,
     catch,
     nbx,
     height,
-    start_x,
     flow,
     fresh,
     part,
@@ -295,13 +296,15 @@
     slot = 128 * line + lane
     place = jnp.minimum(jnp.maximum(slot + shift, 0), ELEMS - 1)
     element = jnp.where(slot < limit, look_up(order[...], place), -1)
-    tall = jnp.concatenate([element.astype(F32), jnp.zeros((112, 128), F32)], axis=0)
+    tall = jnp.concatenate([element >> 7, element & 127, jnp.zeros((96, 128), I32)], axis=0).astype(F32)
     tall = jnp.transpose(tall)
     for l in range(LEVELS):
         for t in range(3):
             n = 3 * l + t
             erow[l, :, 128 * t : 128 * t + 128] = element[n : n + 1]
-            ecol[l, 128 * t : 128 * t + 128] = jnp.broadcast_to(tall[:, n : n + 1], (128, 128))
+            here = slice(128 * t, 128 * t + 128)
+            ehi[l, here] = jnp.broadcast_to(tall[:, n : n + 1], (128, 128)).astype(BF16)
+            elo[l, here] = jnp.broadcast_to(tall[:, n + 16 : n + 17], (128, 128)).astype(BF16)
     line = lax.broadcasted_iota(I32, (8, ELEMS), 0)
     extra = jnp.where(line == 0, jnp.broadcast_to(pattern[...], (8, ELEMS)), 0)
     near = neighbours[...]
@@ -318,6 +321,17 @@
         for k in range(DEG):
             ps.append(ps[k] * h)
         return ps
+
+    def by_face(got):
+        his = [got[:TP, BLOCK * f : BLOCK * f + BLOCK] for f in range(FACES)]
+        los = [got[TP:, BLOCK * f : BLOCK * f + BLOCK] for f in range(FACES)]
+        return jnp.concatenate(his + his + los, axis=0)
+
+    def traces(os, hs):
+        o = os[0:TP]
+        for k in range(1, DEG + 1):
+            o += os[TP * k : TP * k + TP] * (hs[k] * COEF[k])
+        return o
 
     def finish(l):
         x = loaded[...]
@@ -330,17 +344,17 @@
                 y += u * (hs[k] * COEF[k])
             v += u * (hs[k] * COEF[HALF + k])
         y += dot(a3[CP * (HALF - 1) :], right3(v * hs[HALF]))
-        hl = jnp.concatenate(hi_lo(y), axis=0)
+        ends[:, BLOCK * l : BLOCK * l + BLOCK] = jnp.concatenate(hi_lo(y), axis=0)
+
+    def put(first, last, add):
+        here = slice(BLOCK * first, BLOCK * last)
         for n in range(ELEMS // KB):
-            here = slice(KB * n, KB * n + KB)
-            got = dot(hl, scatter[:, here])
+            got = dot(ends[:, here], scatter[here, KB * n : KB * n + KB])
             got = got[:COMP] + got[CP : CP + COMP]
             for t in range(KB // 128):
-                place = pl.ds(n * (KB // 128) + t, COMP, stride=8)
-                if l == 0:
-                    out[place] = got[:, 128 * t : 128 * t + 128]
-                else:
-                    out[place] += got[:, 128 * t : 128 * t + 128]
+                place = pl.ds(n * (KB // 128) + t, COMP, stride=TILES)
+                piece = got[:, 128 * t : 128 * t + 128]
+                out[place] = out[place] + piece if add else piece
 
     for l in range(LEVELS):
         if l > 0:
@@ -348,14 +362,15 @@
             ones = jnp.ones((16, BLOCK), BF16)
             for n in range(ELEMS // KB):
                 here = slice(KB * n, KB * n + KB)
-                got = dot(jnp.concatenate([fresh[...], ones], axis=0), scatter[:, here])
+                back = scatter[BLOCK * (l - 1) : BLOCK * l, here]
+                got = dot(jnp.concatenate([fresh[...], ones], axis=0), back)
                 keep = jnp.broadcast_to(1.0 - got[2 * TP : 2 * TP + 1], (2 * TP, KB))
                 flow[:, here] = (flow[:, here].astype(F32) * keep + got[: 2 * TP]).astype(BF16)
 
         moved = jnp.zeros((2 * CP + 16, BLOCK), F32)
         for m in range(ELEMS // KB):
             moved += dot(rows[:, KB * m : KB * m + KB], one_hot(erow[l], KB * m))
-        start_x[...] = moved[:CP] + moved[CP : 2 * CP]
+        loaded[...] = moved[:CP] + moved[CP : 2 * CP]
         numbers = moved[2 * CP :].astype(I32)
         near = numbers[0:4] * 256 + numbers[4:8]
         for f in range(FACES):
@@ -371,45 +386,45 @@
             acc = jnp.zeros((2 * TP, 2 * KB), F32)
             for m in range(ELEMS // KB):
                 acc += dot(flow[:, KB * m : KB * m + KB], one_hot(row, KB * m))
-            gath[:, here] = acc
+            gath[:, here] = acc.astype(BF16)
             for m in range(SLOTS // KB):
                 catch[KB * m : KB * m + KB, here] = one_hot(row, ELEMS + KB * m)
-        for t in range(ELEMS // 128):
-            row = lax.broadcasted_iota(I32, (BLOCK, 128), 1).astype(F32) + 128.0 * t
-            hit = jnp.where(ecol[l] == row, 1.0, 0.0).astype(BF16)
-            scatter[:, 128 * t : 128 * t + 128] = hit
+        loaded[...] += dot(l3[...], by_face(gath[...]))
+        one, none = jnp.bfloat16(1), jnp.bfloat16(0)
+        lane = lax.broadcasted_iota(I32, (BLOCK, 128), 1).astype(F32).astype(BF16)
+        same = jnp.where(elo[l] == lane, one, none)
+        for t in range(TILES):
+            hit = jnp.where(ehi[l] == jnp.bfloat16(t), same, none)
+            scatter[BLOCK * l : BLOCK * l + BLOCK, 128 * t : 128 * t + 128] = hit
         if l < LEVELS - 1:
             got = dot(flow[...], listed[...])
             for d in range(4):
-                row = sends[:, BND * d : BND * d + BND].astype(F32)
-                hit = jnp.where(ecol[l] == jnp.broadcast_to(row, (BLOCK, BND)), 1.0, 0.0)
-                pick[:, BND * d : BND * d + BND] = hit.astype(BF16)
+                row = sends[:, BND * d : BND * d + BND]
+                row = [
+                    jnp.broadcast_to(digit.astype(F32).astype(BF16), (BLOCK, BND))
+                    for digit in (row >> 7, row & 127)
+                ]
+                hit = jnp.where(elo[l] == row[1], one, none)
+                pick[:, BND * d : BND * d + BND] = jnp.where(ehi[l] == row[0], hit, none)
             gone = dot(jnp.ones((16, BLOCK), BF16), pick[...])[0:1]
             part[...] = got * jnp.broadcast_to(1.0 - gone, (2 * TP, SLOTS))
+        if l == LEVELS - 1:
+            put(0, l, False)
         drain(l)
         arrive(l)
-        come = jnp.concatenate([rb[l, d] for d in range(4)], axis=1)
-        come = dot(jnp.concatenate(hi_lo(come), axis=0), catch[...])
-        his, los = [], []
-        for f in range(FACES):
-            here = slice(BLOCK * f, BLOCK * f + BLOCK)
-            acc = (gath[:, here] + come[:, here]).astype(BF16)
-            his.append(acc[:TP])
-            los.append(acc[TP:])
-        x = start_x[...] + dot(l3[...], jnp.concatenate(his + his + los, axis=0))
+        got = jnp.concatenate([rb[l, d] for d in range(4)], axis=1)
+        got = dot(jnp.concatenate(hi_lo(got), axis=0), catch[...]).astype(BF16)
+        x = loaded[...] + dot(l3[...], by_face(got))
         loaded[...] = x
         if l < LEVELS - 1:
-            x3 = right3(x)
-            hs = powers(l)
-            o = dot(t3[0:TP], x3)
-            for k in range(1, DEG + 1):
-                o += dot(t3[TP * k : TP * k + TP], x3) * (hs[k] * COEF[k])
+            o = traces(dot(t3[...], right3(x)), powers(l))
             o = jnp.concatenate(hi_lo(o), axis=0)
             fresh[...] = o
             fill_sends(l + 1, part[...] + dot(o, pick[...]))
             start(l + 1)
 
     finish(LEVELS - 1)
+    put(LEVELS - 1, LEVELS, True)
 
 def solution(mesh):
     secs, rads = mesh.shape["sector"], mesh.shape["radial"]
@@ -459,18 +474,19 @@
                 pltpu.VMEM((CP, 3 * FACES * TP), BF16),
                 pltpu.VMEM((2 * CP + 16, ELEMS), BF16),
                 pltpu.VMEM((LEVELS, 1, BLOCK), I32),
-                pltpu.VMEM((LEVELS, BLOCK, 128), F32),
-                pltpu.VMEM((BLOCK, ELEMS), BF16),
+                pltpu.VMEM((LEVELS, BLOCK, 128), BF16),
+                pltpu.VMEM((LEVELS, BLOCK, 128), BF16),
+                pltpu.VMEM((LEVELS * BLOCK, ELEMS), BF16),
+                pltpu.VMEM((2 * CP, LEVELS * BLOCK), BF16),
                 pltpu.VMEM((BLOCK, SLOTS), BF16),
                 pltpu.VMEM((ELEMS, SLOTS), BF16),
                 pltpu.VMEM((SLOTS, FACES * BLOCK), BF16),
                 pltpu.VMEM((1, FACES * BLOCK), I32),
                 pltpu.VMEM((LEVELS, 1, BLOCK), F32),
-                pltpu.VMEM((CP, BLOCK), F32),
                 pltpu.VMEM((2 * TP, ELEMS), BF16),
                 pltpu.VMEM((2 * TP, BLOCK), BF16),
                 pltpu.VMEM((2 * TP, SLOTS), F32),
-                pltpu.VMEM((2 * TP, FACES * BLOCK), F32),
+                pltpu.VMEM((2 * TP, FACES * BLOCK), BF16),
                 pltpu.VMEM((CP, BLOCK), F32),
                 pltpu.VMEM((LEVELS, 4, TP, BND), F32),
                 pltpu.VMEM((LEVELS, 4, TP, BND), F32),

time: 35.1 us -> 34.9 us (level)
  no operation moved by 1% of the time
where the time goes in v4:
time: 34.9 us; the launch traced here: 34.7 us
  Pallas kernels  33.9 us (97%)
  local copies, waits for them, and re-layouts  0.81 us (2%)
    pallas_call x1, Pallas kernels, body(): pl.pallas_call(functools.partial(kernel, secs, rads), out_shape=jax.Shape...  33.9 us
    unnamed x1, local copies, waits for them, and re-layouts  0.81 us

profile of v4, /device:TPU:2, one launch (start us, length us, event | category | flops | bytes accessed | tf_op | source)
XLA Modules:
  0.0 34.7 jit_solution(4484781162030461111)
XLA Ops:
  0.0 33.9 %tent_layer.1 = f32[1120,128]{1,0:T(8,128)S(1)} custom-call(f32[1120,128]{1,0:T(8,128)} %bitcast.9, s32[1,1024]{1,0:T(1,128)} %bitcast.12, s32[1,1024]{1,0:T(1,128)} %bitcast.13, s32[4]{0:T(128)} %bitcast.15, s32[4,1024]{1,0:T(4,128)} %bitcast.11, s32[1,512]{1,0:T(1,128)} %bitcast.14, f32[140,140]{1,0:T(8,128)} %operator_hbm.1, f32[60,140]{1,0:T(8,128)} %trace_hbm.1, ...), custom_call_target="tpu_custom_call" | custom-call | tf_op jit(solution)/shard_map/tent_layer/pallas_call | solution.py:461
  33.9 0.8 %copy.14 = f32[1,1,140,1024]{3,1,2,0:T(1,128)} copy(f32[1,1,140,1024]{3,1,2,0:T(1,128)S(1)} %bitcast.8) | data formatting | bytes 1146880

commit v5 on v4

--- a/solution.py
+++ b/solution.py
@@ -116,6 +116,7 @@
     elo,
     scatter,
     ends,
+    sofar,
     pick,
     listed,
     catch,
@@ -350,11 +351,14 @@
         here = slice(BLOCK * first, BLOCK * last)
         for n in range(ELEMS // KB):
             got = dot(ends[:, here], scatter[here, KB * n : KB * n + KB])
-            got = got[:COMP] + got[CP : CP + COMP]
+            got = got[:CP] + got[CP:]
+            if not add:
+                sofar[:, KB * n : KB * n + KB] = got
+                continue
+            got = (sofar[:, KB * n : KB * n + KB] + got)[:COMP]
             for t in range(KB // 128):
                 place = pl.ds(n * (KB // 128) + t, COMP, stride=TILES)
-                piece = got[:, 128 * t : 128 * t + 128]
-                out[place] = out[place] + piece if add else piece
+                out[place] = got[:, 128 * t : 128 * t + 128]
 
     for l in range(LEVELS):
         if l > 0:
@@ -478,6 +482,7 @@
                 pltpu.VMEM((LEVELS, BLOCK, 128), BF16),
                 pltpu.VMEM((LEVELS * BLOCK, ELEMS), BF16),
                 pltpu.VMEM((2 * CP, LEVELS * BLOCK), BF16),
+                pltpu.VMEM((CP, ELEMS), F32),
                 pltpu.VMEM((BLOCK, SLOTS), BF16),
                 pltpu.VMEM((ELEMS, SLOTS), BF16),
                 pltpu.VMEM((SLOTS, FACES * BLOCK), BF16),

time: 34.9 us -> 34.8 us (level)
  no operation moved by 1% of the time
where the time goes in v5:
time: 34.8 us; the launch traced here: 34.7 us
  Pallas kernels  33.9 us (97%)
  local copies, waits for them, and re-layouts  0.81 us (2%)
    pallas_call x1, Pallas kernels, body(): pl.pallas_call(functools.partial(kernel, secs, rads), out_shape=jax.Shape...  33.9 us
    unnamed x1, local copies, waits for them, and re-layouts  0.81 us

profile of v5, /device:TPU:2, one launch (start us, length us, event | category | flops | bytes accessed | tf_op | source)
XLA Modules:
  0.0 34.7 jit_solution(8559535249802390360)
XLA Ops:
  0.0 33.9 %tent_layer.1 = f32[1120,128]{1,0:T(8,128)S(1)} custom-call(f32[1120,128]{1,0:T(8,128)} %bitcast.9, s32[1,1024]{1,0:T(1,128)} %bitcast.12, s32[1,1024]{1,0:T(1,128)} %bitcast.13, s32[4]{0:T(128)} %bitcast.15, s32[4,1024]{1,0:T(4,128)} %bitcast.11, s32[1,512]{1,0:T(1,128)} %bitcast.14, f32[140,140]{1,0:T(8,128)} %operator_hbm.1, f32[60,140]{1,0:T(8,128)} %trace_hbm.1, ...), custom_call_target="tpu_custom_call" | custom-call | tf_op jit(solution)/shard_map/tent_layer/pallas_call | solution.py:465
  33.9 0.8 %copy.14 = f32[1,1,140,1024]{3,1,2,0:T(1,128)} copy(f32[1,1,140,1024]{3,1,2,0:T(1,128)S(1)} %bitcast.8) | data formatting | bytes 1146880
